TPU v7x, 32 devices: a whole 2x2x4 slice. The times are simulated.
32 devices in a mesh: cols: 8 (over z, y), chan: 4 (over x, core).
Axes of the slice: x: 2, y: 2, z: 4, core: 2. Of those that a mesh axis runs over, the one named last changes fastest.
Arguments:
- anomaly: bfloat16 [2048, 80, 128], P('cols'), may hold values from -6 to 6
- jacobian: bfloat16 [1024, 256, 128], P(('cols', 'chan')), may hold values from -0.5 to 0.5
- foot_cols: int32 [1024, 4], P('cols'), may hold values from 0 to 2047, as said below
- foot_weight: float32 [1024, 4], P('cols'), may hold values from 0.1 to 1
- obs_count: int32 [8], P('cols'), may hold values from 32 to 128, as said below
- obs_weight: bfloat16 [256, 1024], P(None, ('cols', 'chan')), may hold values from 0.25 to 4
Outputs:
- radiance_pert: bfloat16 [80, 256, 1024], P(None, 'chan', 'cols')
- ensemble_gram: float32 [64, 80, 80], P('cols', 'chan')
Inputs may be any that keep to these rules, and one draw needn't show every extreme that they name: `foot_cols`: the footprint columns of an observation of tile t lie among the columns t * 256 - 32 to (t + 1) * 256 + 31, taken modulo 2048. The live observations of tile t are its first obs_count[t] slots; in every draw at least one tile has all 128 slots live.
All inputs are finite; a program needn't handle non-finite values.
Results may differ from a plain program's by a relative error of at most 0.0095.
Values may be sent and summed in bfloat16 or wider, within the bound.
A program may use at most 64 MiB of HBM per device.

v0:
```python
import jax
import jax.numpy as jnp
from jax import lax
from jax.sharding import PartitionSpec as P

CH = 256
OBS_DEV = 128
HALO = 32
PTS = 8


def extended_2(block, sides, width):
    for axis, dim in sides:
        count = lax.axis_size(axis)
        forward = [(i, i + 1) for i in range(count - 1)]
        forward.append((count - 1, 0))
        backward = [(target, source) for source, target in forward]
        low = lax.ppermute(
            lax.slice_in_dim(block, block.shape[dim] - width, None, axis=dim), axis, forward
        )
        high = lax.ppermute(lax.slice_in_dim(block, 0, width, axis=dim), axis, backward)
        block = jnp.concatenate([low, block, high], axis=dim)
    return block


def taper(distance, half_width):
    relative = jnp.abs(distance) / half_width
    near_part = (
        ((-0.25 * relative + 0.5) * relative + 0.625) * relative - 5.0 / 3.0
    ) * relative * relative + 1.0
    bounded = jnp.maximum(relative, 1.0)
    far_part = (
        ((((relative / 12.0 - 0.5) * relative + 0.625) * relative + 5.0 / 3.0) * relative - 5.0)
        * relative
        + 4.0
        - 2.0 / (3.0 * bounded)
    )
    return jnp.where(relative <= 1.0, near_part, jnp.where(relative <= 2.0, far_part, 0.0))


def local_gram(perturbed, error_weight, centers, tile_cols):
    spacing = tile_cols / PTS
    points = (jnp.arange(PTS, dtype=jnp.float32) + 0.5) * spacing
    locality = taper(centers[None, :] - points[:, None], spacing)
    weighted = perturbed.astype(jnp.float32) * error_weight.astype(jnp.float32)
    flat_values = perturbed.reshape(perturbed.shape[0], -1)
    gram_list = []
    for point_index in range(PTS):
        scaled = (weighted * locality[point_index][None, None, :]).astype(jnp.bfloat16)
        flat_scaled = scaled.reshape(perturbed.shape[0], -1)
        gram_list.append(
            jnp.einsum("mx,kx->mk", flat_scaled, flat_values, preferred_element_type=jnp.float32)
        )
    return jnp.stack(gram_list) / (CH * OBS_DEV)


def shards(anomaly, jacobian, foot_cols, foot_weight, obs_count, obs_weight):
    col_groups = lax.axis_size("cols")
    tile_index = lax.axis_index("cols")
    chan_index = lax.axis_index("chan")
    tile_cols = anomaly.shape[0]
    obs_share = jacobian.shape[0]
    extended = extended_2(anomaly, (("cols", 0),), HALO)
    offsets = jnp.mod(foot_cols - tile_index * tile_cols + HALO, tile_cols * col_groups)
    centers = jnp.sum(foot_weight * (offsets - HALO).astype(jnp.float32), axis=1) / jnp.sum(
        foot_weight, axis=1
    )
    first_obs = chan_index * obs_share
    own_offsets = lax.dynamic_slice_in_dim(offsets, first_obs, obs_share, 0)
    own_gains = lax.dynamic_slice_in_dim(foot_weight, first_obs, obs_share, 0)
    mixed_cols = jnp.zeros((obs_share, anomaly.shape[1], anomaly.shape[2]), jnp.float32)
    for column_slot in range(own_offsets.shape[1]):
        mixed_cols = mixed_cols + own_gains[:, column_slot, None, None] * extended[
            own_offsets[:, column_slot]
        ].astype(jnp.float32)
    mixed_cols = mixed_cols.astype(jnp.bfloat16)
    radiance = jnp.einsum("ncl,nml->mcn", jacobian, mixed_cols, preferred_element_type=jnp.float32)
    slot_numbers = first_obs + jnp.arange(obs_share, dtype=jnp.int32)
    live_mask = (slot_numbers < obs_count[0]).astype(jnp.float32)
    perturbed = (radiance * live_mask[None, None, :]).astype(jnp.bfloat16)
    error_weight = obs_weight[None]
    own_centers = lax.dynamic_slice_in_dim(centers, first_obs, obs_share, 0)
    partial_gram = local_gram(perturbed, error_weight, own_centers, tile_cols)
    received = lax.all_to_all(perturbed, "chan", split_axis=1, concat_axis=2, tiled=True)
    gram_rows = lax.psum_scatter(
        partial_gram.astype(jnp.bfloat16), "chan", scatter_dimension=1, tiled=True
    ).astype(jnp.float32)
    return (received, gram_rows)


def solution(mesh):
    return jax.shard_map(
        shards,
        mesh=mesh,
        in_specs=(
            P("cols", None, None),
            P(("cols", "chan"), None, None),
            P("cols", None),
            P("cols", None),
            P("cols"),
            P(None, ("cols", "chan")),
        ),
        out_specs=(P(None, "chan", "cols"), P("cols", "chan", None)),
        check_vma=False,
    )
```

profile of v0, /device:TPU:0, one launch (start us, length us, event | category | flops | bytes accessed | tf_op | source)
XLA Modules:
  0.0 120.4 jit_solution(7480939596906263955)
XLA Ops:
  7.2 0.0 copy-start
  7.2 0.0 copy-start.2
  7.2 0.0 copy-start.3
  7.2 0.0 copy-start.1
  7.2 1.5 %fusion.54 = (bf16[32,80,128]{2,1,0:T(8,128)(2,1)S(1)}, bf16[32,80,128]{2,1,0:T(8,128)(2,1)S(1)}) fusion(bf16[256,80,128]{2,1,0:T(8,128)(2,1)} %param.6), kind=kLoop, calls=%fused_computation.105 | loop fusion | bytes 2621440 | tf_op jit(solution)/shard_map/slice | solution.py:21
  8.7 3.0 %collective-permute-start = (bf16[32,80,128]{2,1,0:T(8,128)(2,1)S(1)}, bf16[32,80,128]{2,1,0:T(8,128)(2,1)}, u32[]{:S(2)}, u32[]{:S(2)}) collective-permute-start(bf16[32,80,128]{2,1,0:T(8,128)(2,1)S(1)} %get-tuple-element.12), channel_id=1, source_target_pairs={{0,4},{4,8},{8,12},{12,16},{16,20},{20,24},{24,28},{28,0},{1,5},{5... | collective-permute-start | bytes 1966088 | tf_op jit(solution)/shard_map/ppermute | solution.py:18
  11.8 3.1 %collective-permute-start.1 = (bf16[32,80,128]{2,1,0:T(8,128)(2,1)S(1)}, bf16[32,80,128]{2,1,0:T(8,128)(2,1)}, u32[]{:S(2)}, u32[]{:S(2)}) collective-permute-start(bf16[32,80,128]{2,1,0:T(8,128)(2,1)S(1)} %get-tuple-element.11), channel_id=1, source_target_pairs={{4,0},{8,4},{12,8},{16,12},{20,16},{24,20},{28,24},{0,28},{5,1},{9... | collective-permute-start | bytes 1966088 | tf_op jit(solution)/shard_map/ppermute | solution.py:21
  15.5 0.0 copy-done.2
  15.5 0.1 constant_dynamic-slice_fusion.1
  15.6 0.0 copy-done.3
  15.7 0.1 constant_dynamic-slice_fusion
  15.8 0.1 dynamic_slice.11
  15.8 0.0 copy-done.1
  15.9 0.1 fusion.46
  16.0 23.8 %collective-permute-done = bf16[32,80,128]{2,1,0:T(8,128)(2,1)} collective-permute-done((bf16[32,80,128]{2,1,0:T(8,128)(2,1)S(1)}, bf16[32,80,128]{2,1,0:T(8,128)(2,1)}, u32[]{:S(2)}, u32[]{:S(2)}) %collective-permute-start) | collective-permute-done | bytes 655392 | tf_op jit(solution)/shard_map/ppermute | solution.py:18
  39.8 2.0 %constant_dynamic-update-slice_fusion.2 = bf16[320,80,128]{2,1,0:T(8,128)(2,1)} fusion(bf16[32,80,128]{2,1,0:T(8,128)(2,1)} %collective-permute-done), kind=kLoop, calls=%fused_computation.63 | loop fusion | bytes 1310720
  41.8 5.7 %constant_dynamic-update-slice_fusion.1 = bf16[320,80,128]{2,1,0:T(8,128)(2,1)} fusion(bf16[320,80,128]{2,1,0:T(8,128)(2,1)} %constant_dynamic-update-slice_fusion.2, bf16[256,80,128]{2,1,0:T(8,128)(2,1)} %param.6), kind=kLoop, calls=%fused_computation.62 | loop fusion | bytes 10485760
  47.5 0.0 collective-permute-done.1
  47.5 2.0 %constant_dynamic-update-slice_fusion = bf16[320,80,128]{2,1,0:T(8,128)(2,1)} fusion(bf16[320,80,128]{2,1,0:T(8,128)(2,1)} %constant_dynamic-update-slice_fusion.1, bf16[32,80,128]{2,1,0:T(8,128)(2,1)} %collective-permute-done.1), kind=kLoop, calls=%fused_computation.61 | loop fusion | bytes 1310720 | tf_op jit(solution)/shard_map/concatenate | solution.py:22
  49.5 4.3 %gather_fusion.3 = bf16[32,80,128]{2,1,0:T(8,128)(2,1)} fusion(bf16[320,80,128]{2,1,0:T(8,128)(2,1)} %constant_dynamic-update-slice_fusion, s32[1024]{0:T(1024)S(1)} %get-tuple-element.29), kind=kCustom, calls=%fused_computation.3 | custom fusion | bytes 1310848 | tf_op jit(solution)/shard_map/gather | solution.py:73
  53.8 4.4 %gather_fusion.2 = bf16[32,80,128]{2,1,0:T(8,128)(2,1)} fusion(bf16[320,80,128]{2,1,0:T(8,128)(2,1)} %constant_dynamic-update-slice_fusion, s32[1024]{0:T(1024)S(1)} %get-tuple-element.30), kind=kCustom, calls=%fused_computation.2 | custom fusion | bytes 1310848 | tf_op jit(solution)/shard_map/gather | solution.py:73
  58.2 4.3 %gather_fusion.1 = bf16[32,80,128]{2,1,0:T(8,128)(2,1)} fusion(bf16[320,80,128]{2,1,0:T(8,128)(2,1)} %constant_dynamic-update-slice_fusion, s32[1024]{0:T(1024)S(1)} %get-tuple-element.31), kind=kCustom, calls=%fused_computation.1 | custom fusion | bytes 1310848 | tf_op jit(solution)/shard_map/gather | solution.py:73
  62.5 4.4 %gather_fusion = bf16[32,80,128]{2,1,0:T(8,128)(2,1)} fusion(bf16[320,80,128]{2,1,0:T(8,128)(2,1)} %constant_dynamic-update-slice_fusion, s32[1024]{0:T(1024)S(1)} %get-tuple-element.32), kind=kCustom, calls=%fused_computation | custom fusion | bytes 1310848 | tf_op jit(solution)/shard_map/gather | solution.py:73
  66.9 0.0 copy-done
  66.9 2.6 %fusion.8 = bf16[80,256,32]{1,0,2:T(8,128)(2,1)S(1)} fusion(bf16[32,256,128]{2,1,0:T(8,128)(2,1)S(1)} %copy-done, f32[32]{0:T(128)S(1)} %compare_convert_fusion, bf16[32,80,128]{2,1,0:T(8,128)(2,1)} %gather_fusion.3, bf16[32,80,128]{2,1,0:T(8,128)(2,1)} %gather_fusion.2, bf16[32,80,128]{2,1,0:T(8,128)(2,1)} %gather_fusion.1, ...), kind=kOutput, calls=%fused_computation.22 | convolution fusion | flops 173015040 | bytes 6029952 | tf_op jit(solution)/shard_map/ncl,nml->mcn/dot_general | solution.py:77
  69.5 3.0 %copy.14 = bf16[80,256,32]{0,2,1:T(8,128)(2,1)} copy(bf16[80,256,32]{1,0,2:T(8,128)(2,1)S(1)} %fusion.8) | data formatting | bytes 2621440 | tf_op jit(solution)/shard_map/convert_element_type | solution.py:80
  72.5 4.4 %all-to-all-start = ((bf16[80,256,32]{0,2,1:T(8,128)(2,1)}), bf16[80,256,32]{0,2,1:T(8,128)(2,1)}, u32[]{:S(2)}, u32[]{:S(2)}) async-start(bf16[80,256,32]{0,2,1:T(8,128)(2,1)} %copy.14), calls=%async_computation | async-start | bytes 4194304 | tf_op jit(solution)/shard_map/all_to_all | solution.py:84
  76.9 0.0 reduce-scatter.2.cloned.1.call-start
  77.0 0.6 fusion.40
  77.6 0.6 fusion.38
  78.1 0.6 fusion.36
  78.7 0.6 fusion.34
  79.2 0.6 fusion.32
  79.8 0.6 fusion.30
  80.4 0.6 fusion.28
  80.9 0.6 fusion.26
  81.5 0.7 copy.16
  82.2 0.0 reduce-scatter.2.cloned.1.call-update
  82.3 22.6 %reduce-scatter.2.cloned.1.call-done = bf16[8,20,80]{2,0,1:T(8,128)(2,1)} async-done(((bf16[8,80,80]{2,0,1:T(8,128)(2,1)}), bf16[8,20,80]{2,0,1:T(8,128)(2,1)}) %reduce-scatter.2.cloned.1.call-update) | async-done | bytes 25616 | tf_op jit(solution)/shard_map/reduce_scatter | solution.py:85
  104.9 1.4 %convert_element_type.88 = f32[8,20,80]{2,0,1:T(8,128)} convert(bf16[8,20,80]{2,0,1:T(8,128)(2,1)} %reduce-scatter.2.cloned.1.call-done) | non-fusion elementwise | flops 12800 | bytes 76800 | tf_op jit(solution)/shard_map/convert_element_type | solution.py:87
  106.3 0.0 all-to-all-done
  106.3 3.6 %copy.15 = bf16[80,64,4,32]{0,3,2,1:T(8,128)(2,1)} copy(bf16[80,64,4,32]{0,3,1,2:T(8,128)(2,1)} %bitcast.11) | data formatting | bytes 2621440 | tf_op jit(solution)/shard_map/all_to_all | solution.py:84
  109.9 3.7 %copy.17 = bf16[80,64,128]{2,1,0:T(8,128)(2,1)} copy(bf16[80,64,128]{0,2,1:T(8,128)(2,1)} %bitcast.89) | data formatting | bytes 2621440
  (11 shorter events, 0.1 us)
Async XLA Ops:
  7.2 59.7 %copy-start = (bf16[32,256,128]{2,1,0:T(8,128)(2,1)S(1)}, bf16[32,256,128]{2,1,0:T(8,128)(2,1)}, u32[]{:S(2)}) copy-start(bf16[32,256,128]{2,1,0:T(8,128)(2,1)} %param.7) | copy-start | bytes 6291460
  7.2 8.4 %copy-start.2 = (f32[128,4]{0,1:T(4,128)S(1)}, f32[128,4]{0,1:T(4,128)}, u32[]{:S(2)}) copy-start(f32[128,4]{0,1:T(4,128)} %param.9) | copy-start | bytes 6148
  7.2 8.4 %copy-start.3 = (s32[128,4]{0,1:T(4,128)S(1)}, s32[128,4]{0,1:T(4,128)}, u32[]{:S(2)}) copy-start(s32[128,4]{0,1:T(4,128)} %param.8) | copy-start | bytes 6148
  7.2 8.6 %copy-start.1 = (bf16[256,32]{0,1:T(8,128)(2,1)S(1)}, bf16[256,32]{0,1:T(8,128)(2,1)}, u32[]{:S(2)}) copy-start(bf16[256,32]{0,1:T(8,128)(2,1)} %param.11) | copy-start | bytes 49156
  8.7 31.1 %collective-permute-start = (bf16[32,80,128]{2,1,0:T(8,128)(2,1)S(1)}, bf16[32,80,128]{2,1,0:T(8,128)(2,1)}, u32[]{:S(2)}, u32[]{:S(2)}) collective-permute-start(bf16[32,80,128]{2,1,0:T(8,128)(2,1)S(1)} %get-tuple-element.12), channel_id=1, source_target_pairs={{0,4},{4,8},{8,12},{12,16},{16,20},{20,24},{24,28},{28,0},{1,5},{5... | collective-permute-start | bytes 1966088 | tf_op jit(solution)/shard_map/ppermute | solution.py:18
  11.8 35.7 %collective-permute-start.1 = (bf16[32,80,128]{2,1,0:T(8,128)(2,1)S(1)}, bf16[32,80,128]{2,1,0:T(8,128)(2,1)}, u32[]{:S(2)}, u32[]{:S(2)}) collective-permute-start(bf16[32,80,128]{2,1,0:T(8,128)(2,1)S(1)} %get-tuple-element.11), channel_id=1, source_target_pairs={{4,0},{8,4},{12,8},{16,12},{20,16},{24,20},{28,24},{0,28},{5,1},{9... | collective-permute-start | bytes 1966088 | tf_op jit(solution)/shard_map/ppermute | solution.py:21
  72.5 33.8 %all-to-all-start = ((bf16[80,256,32]{0,2,1:T(8,128)(2,1)}), bf16[80,256,32]{0,2,1:T(8,128)(2,1)}, u32[]{:S(2)}, u32[]{:S(2)}) async-start(bf16[80,256,32]{0,2,1:T(8,128)(2,1)} %copy.14), calls=%async_computation | async-start | bytes 4194304 | tf_op jit(solution)/shard_map/all_to_all | solution.py:84
  76.9 27.9 %reduce-scatter.2.cloned.1.call-start = ((), (), s32[]{:S(2)}) async-start(), calls=%async_computation.2 | async-start | bytes 204800 | tf_op jit(solution)/shard_map/reduce_scatter | solution.py:85
Sparse Core Ops, SparseCore 0:
  82.4 22.4 reduce-scatter.1
where the time goes:
time: 121 us; the launch traced here: 120 us
  waiting for transfers between devices  46.5 us (38%)
  local copies, waits for them, and re-layouts  39.8 us (33%)
  between operations  14.9 us (12%)
  starting transfers between devices  10.6 us (9%)
  matrix products  7.02 us (6%)
  other arithmetic  1.61 us (1%)
    ppermute x1, waiting for transfers between devices, extended_2(): lax.ppermute(lax.slice_in_dim(block, block.shape[dim] - width, None, axis...  23.8 us
    reduce_scatter x1, waiting for transfers between devices, shards(): lax.psum_scatter(partial_gram.astype(jnp.bfloat16), 'chan', scatter_dimen...  22.6 us
    gather x4, local copies, waits for them, and re-layouts, shards(): extended[own_offsets[:, column_slot]].astype(jnp.float32)  17.4 us
    unnamed x11, local copies, waits for them, and re-layouts  11.4 us
    all_to_all x1, starting transfers between devices, shards(): lax.all_to_all(perturbed, 'chan', split_axis=1, concat_axis=2, tiled=True)  4.45 us
    dot_general x8, matrix products, local_gram(): jnp.einsum('mx,kx->mk', flat_scaled, flat_values, preferred_element_type=...  4.43 us
    all_to_all x1, local copies, waits for them, and re-layouts, shards(): lax.all_to_all(perturbed, 'chan', split_axis=1, concat_axis=2, tiled=True)  3.56 us
    ppermute x1, starting transfers between devices, extended_2(): lax.ppermute(lax.slice_in_dim(block, 0, width, axis=dim), axis, backward)  3.1 us
  transfers between devices with their start and end apart: 4, of which 2 were waited for; matrix products, arithmetic and copies ran while one was open for 12% of the time, Pallas kernels for 0%

commit v1 on v0

--- a/solution.py
+++ b/solution.py
@@ -81,7 +81,10 @@
     error_weight = obs_weight[None]
     own_centers = lax.dynamic_slice_in_dim(centers, first_obs, obs_share, 0)
     partial_gram = local_gram(perturbed, error_weight, own_centers, tile_cols)
-    received = lax.all_to_all(perturbed, "chan", split_axis=1, concat_axis=2, tiled=True)
+    n_dev = lax.axis_size("chan")
+    parts = jnp.stack(jnp.split(perturbed, n_dev, axis=1), axis=0)
+    parts = lax.all_to_all(parts, "chan", split_axis=0, concat_axis=0)
+    received = jnp.concatenate(parts, axis=2)
     gram_rows = lax.psum_scatter(
         partial_gram.astype(jnp.bfloat16), "chan", scatter_dimension=1, tiled=True
     ).astype(jnp.float32)

time: 121 us -> 126 us (1.041)
  local copies, waits for them, and re-layouts: 39.8 us -> 42.8 us
  other arithmetic: 1.61 us -> 3.81 us
    another operation x0 -> x2, local copies, waits for them, and re-layouts: none -> 5.94 us  [shards(): parts = jnp.stack(jnp.split(perturbed, n_dev, axis=1), axis=0)]
    reshape x0 -> x1, local copies, waits for them, and re-layouts: none -> 3.57 us  [shards(): received = jnp.concatenate(parts, axis=2)]
    all_to_all x1 -> x0, local copies, waits for them, and re-layouts: 3.56 us -> none  [shards(): lax.all_to_all(perturbed, 'chan', split_axis=1, concat_axis=2, tiled=True)]
    convert_element_type x1 -> x0, local copies, waits for them, and re-layouts: 3.02 us -> none  [shards(): perturbed = (radiance * live_mask[None, None, :]).astype(jnp.bfloat16)]
    another operation x0 -> x1, other arithmetic: none -> 2.2 us  [shards(): parts = jnp.stack(jnp.split(perturbed, n_dev, axis=1), axis=0)]
where the time goes in v1:
time: 126 us
  waiting for transfers between devices  46.5 us (37%)
  local copies, waits for them, and re-layouts  42.8 us (34%)
  between operations  14.9 us (12%)
  starting transfers between devices  10.6 us (8%)
  matrix products  7.01 us (6%)
  other arithmetic  3.81 us (3%)
    ppermute x1, waiting for transfers between devices, extended_2(): lax.ppermute(lax.slice_in_dim(block, block.shape[dim] - width, None, axis...  23.8 us
    reduce_scatter x1, waiting for transfers between devices, shards(): lax.psum_scatter(partial_gram.astype(jnp.bfloat16), 'chan', scatter_dimen...  22.6 us
    gather x4, local copies, waits for them, and re-layouts, shards(): extended[own_offsets[:, column_slot]].astype(jnp.float32)  17.4 us
    unnamed x11, local copies, waits for them, and re-layouts  11.4 us
    another operation x2, local copies, waits for them, and re-layouts, shards(): parts = jnp.stack(jnp.split(perturbed, n_dev, axis=1), axis=0)  5.94 us
    all_to_all x1, starting transfers between devices, shards(): parts = lax.all_to_all(parts, 'chan', split_axis=0, concat_axis=0)  4.44 us
    dot_general x8, matrix products, local_gram(): jnp.einsum('mx,kx->mk', flat_scaled, flat_values, preferred_element_type=...  4.42 us
    reshape x1, local copies, waits for them, and re-layouts, shards(): received = jnp.concatenate(parts, axis=2)  3.57 us
  transfers between devices with their start and end apart: 4, of which 2 were waited for; matrix products, arithmetic and copies ran while one was open for 12% of the time, Pallas kernels for 0%

profile of v1, /device:TPU:0, one launch (start us, length us, event | category | flops | bytes accessed | tf_op | source)
XLA Modules:
  0.0 125.6 jit_solution(4361788523839178280)
XLA Ops:
  7.2 0.0 copy-start
  7.2 0.0 copy-start.2
  7.2 0.0 copy-start.3
  7.2 0.0 copy-start.1
  7.2 1.5 %fusion.54 = (bf16[32,80,128]{2,1,0:T(8,128)(2,1)S(1)}, bf16[32,80,128]{2,1,0:T(8,128)(2,1)S(1)}) fusion(bf16[256,80,128]{2,1,0:T(8,128)(2,1)} %param.6), kind=kLoop, calls=%fused_computation.110 | loop fusion | bytes 2621440 | tf_op jit(solution)/shard_map/slice | solution.py:21
  8.7 3.0 %collective-permute-start = (bf16[32,80,128]{2,1,0:T(8,128)(2,1)S(1)}, bf16[32,80,128]{2,1,0:T(8,128)(2,1)}, u32[]{:S(2)}, u32[]{:S(2)}) collective-permute-start(bf16[32,80,128]{2,1,0:T(8,128)(2,1)S(1)} %get-tuple-element.10), channel_id=1, source_target_pairs={{0,4},{4,8},{8,12},{12,16},{16,20},{20,24},{24,28},{28,0},{1,5},{5... | collective-permute-start | bytes 1966088 | tf_op jit(solution)/shard_map/ppermute | solution.py:18
  11.8 3.1 %collective-permute-start.1 = (bf16[32,80,128]{2,1,0:T(8,128)(2,1)S(1)}, bf16[32,80,128]{2,1,0:T(8,128)(2,1)}, u32[]{:S(2)}, u32[]{:S(2)}) collective-permute-start(bf16[32,80,128]{2,1,0:T(8,128)(2,1)S(1)} %get-tuple-element.9), channel_id=1, source_target_pairs={{4,0},{8,4},{12,8},{16,12},{20,16},{24,20},{28,24},{0,28},{5,1},{9... | collective-permute-start | bytes 1966088 | tf_op jit(solution)/shard_map/ppermute | solution.py:21
  15.5 0.0 copy-done.2
  15.5 0.1 constant_dynamic-slice_fusion.1
  15.6 0.0 copy-done.3
  15.7 0.1 constant_dynamic-slice_fusion
  15.8 0.1 dynamic_slice.11
  15.8 0.0 copy-done.1
  15.9 0.1 fusion.46
  16.0 23.8 %collective-permute-done = bf16[32,80,128]{2,1,0:T(8,128)(2,1)} collective-permute-done((bf16[32,80,128]{2,1,0:T(8,128)(2,1)S(1)}, bf16[32,80,128]{2,1,0:T(8,128)(2,1)}, u32[]{:S(2)}, u32[]{:S(2)}) %collective-permute-start) | collective-permute-done | bytes 655392 | tf_op jit(solution)/shard_map/ppermute | solution.py:18
  39.8 2.0 %constant_dynamic-update-slice_fusion.2 = bf16[320,80,128]{2,1,0:T(8,128)(2,1)} fusion(bf16[32,80,128]{2,1,0:T(8,128)(2,1)} %collective-permute-done), kind=kLoop, calls=%fused_computation.68 | loop fusion | bytes 1310720
  41.8 5.7 %constant_dynamic-update-slice_fusion.1 = bf16[320,80,128]{2,1,0:T(8,128)(2,1)} fusion(bf16[320,80,128]{2,1,0:T(8,128)(2,1)} %constant_dynamic-update-slice_fusion.2, bf16[256,80,128]{2,1,0:T(8,128)(2,1)} %param.6), kind=kLoop, calls=%fused_computation.67 | loop fusion | bytes 10485760
  47.5 0.0 collective-permute-done.1
  47.5 2.0 %constant_dynamic-update-slice_fusion = bf16[320,80,128]{2,1,0:T(8,128)(2,1)} fusion(bf16[320,80,128]{2,1,0:T(8,128)(2,1)} %constant_dynamic-update-slice_fusion.1, bf16[32,80,128]{2,1,0:T(8,128)(2,1)} %collective-permute-done.1), kind=kLoop, calls=%fused_computation.66 | loop fusion | bytes 1310720 | tf_op jit(solution)/shard_map/concatenate | solution.py:22
  49.5 4.3 %gather_fusion.3 = bf16[32,80,128]{2,1,0:T(8,128)(2,1)} fusion(bf16[320,80,128]{2,1,0:T(8,128)(2,1)} %constant_dynamic-update-slice_fusion, s32[1024]{0:T(1024)S(1)} %get-tuple-element.31), kind=kCustom, calls=%fused_computation.3 | custom fusion | bytes 1310848 | tf_op jit(solution)/shard_map/gather | solution.py:73
  53.8 4.3 %gather_fusion.2 = bf16[32,80,128]{2,1,0:T(8,128)(2,1)} fusion(bf16[320,80,128]{2,1,0:T(8,128)(2,1)} %constant_dynamic-update-slice_fusion, s32[1024]{0:T(1024)S(1)} %get-tuple-element.32), kind=kCustom, calls=%fused_computation.2 | custom fusion | bytes 1310848 | tf_op jit(solution)/shard_map/gather | solution.py:73
  58.2 4.3 %gather_fusion.1 = bf16[32,80,128]{2,1,0:T(8,128)(2,1)} fusion(bf16[320,80,128]{2,1,0:T(8,128)(2,1)} %constant_dynamic-update-slice_fusion, s32[1024]{0:T(1024)S(1)} %get-tuple-element.33), kind=kCustom, calls=%fused_computation.1 | custom fusion | bytes 1310848 | tf_op jit(solution)/shard_map/gather | solution.py:73
  62.5 4.4 %gather_fusion = bf16[32,80,128]{2,1,0:T(8,128)(2,1)} fusion(bf16[320,80,128]{2,1,0:T(8,128)(2,1)} %constant_dynamic-update-slice_fusion, s32[1024]{0:T(1024)S(1)} %get-tuple-element.34), kind=kCustom, calls=%fused_computation | custom fusion | bytes 1310848 | tf_op jit(solution)/shard_map/gather | solution.py:73
  66.9 0.0 copy-done
  66.9 2.6 %fusion.8 = bf16[80,256,32]{1,0,2:T(8,128)(2,1)S(1)} fusion(bf16[32,256,128]{2,1,0:T(8,128)(2,1)S(1)} %copy-done, f32[32]{0:T(128)S(1)} %compare_convert_fusion, bf16[32,80,128]{2,1,0:T(8,128)(2,1)} %gather_fusion.3, bf16[32,80,128]{2,1,0:T(8,128)(2,1)} %gather_fusion.2, bf16[32,80,128]{2,1,0:T(8,128)(2,1)} %gather_fusion.1, ...), kind=kOutput, calls=%fused_computation.23 | convolution fusion | flops 173015040 | bytes 6029952 | tf_op jit(solution)/shard_map/ncl,nml->mcn/dot_general | solution.py:77
  69.5 0.6 slice_bitcast_fusion.3
  70.1 2.2 %pad_maximum_fusion = bf16[4,80,64,32]{2,1,3,0:T(8,128)(2,1)} fusion(bf16[1,80,64,32]{2,1,3,0:T(8,128)(2,1)S(1)} %get-tuple-element.12, bf16[1,80,64,32]{2,1,3,0:T(8,128)(2,1)S(1)} %get-tuple-element.13, bf16[1,80,64,32]{2,1,3,0:T(8,128)(2,1)S(1)} %get-tuple-element.14, bf16[1,80,64,32]{2,1,3,0:T(8,128)(2,1)S(1)} %get-tuple-element.11), kind=kLoop, calls=%fused_computation.4 | loop fusion | flops 1966080 | bytes 2621440 | tf_op jit(solution)/shard_map/stack | solution.py:85
  72.3 5.3 %copy.12 = bf16[4,80,64,32]{1,3,2,0:T(8,128)(2,1)} copy(bf16[4,80,64,32]{2,1,3,0:T(8,128)(2,1)} %pad_maximum_fusion) | data formatting | bytes 2621440 | tf_op jit(solution)/shard_map/stack | solution.py:85
  77.6 4.4 %all-to-all-start = ((bf16[4,80,64,32]{1,3,2,0:T(8,128)(2,1)}), bf16[4,80,64,32]{1,3,2,0:T(8,128)(2,1)}, u32[]{:S(2)}, u32[]{:S(2)}) async-start(bf16[4,80,64,32]{1,3,2,0:T(8,128)(2,1)} %copy.12), calls=%async_computation | async-start | bytes 4194304 | tf_op jit(solution)/shard_map/all_to_all | solution.py:86
  82.1 0.0 reduce-scatter.2.cloned.1.call-start
  82.1 0.6 fusion.40
  82.7 0.6 fusion.38
  83.2 0.6 fusion.36
  83.8 0.5 fusion.34
  84.4 0.6 fusion.32
  84.9 0.6 fusion.30
  85.5 0.6 fusion.28
  86.0 0.6 fusion.26
  86.6 0.7 copy.14
  87.4 0.0 reduce-scatter.2.cloned.1.call-update
  87.4 22.6 %reduce-scatter.2.cloned.1.call-done = bf16[8,20,80]{2,0,1:T(8,128)(2,1)} async-done(((bf16[8,80,80]{2,0,1:T(8,128)(2,1)}), bf16[8,20,80]{2,0,1:T(8,128)(2,1)}) %reduce-scatter.2.cloned.1.call-update) | async-done | bytes 25616 | tf_op jit(solution)/shard_map/reduce_scatter | solution.py:88
  110.0 1.4 %convert_element_type.88 = f32[8,20,80]{2,0,1:T(8,128)} convert(bf16[8,20,80]{2,0,1:T(8,128)(2,1)} %reduce-scatter.2.cloned.1.call-done) | non-fusion elementwise | flops 12800 | bytes 76800 | tf_op jit(solution)/shard_map/convert_element_type | solution.py:90
  111.4 0.0 all-to-all-done
  111.4 3.6 %copy.13 = bf16[80,64,4,32]{0,3,2,1:T(8,128)(2,1)} copy(bf16[80,64,4,32]{0,3,1,2:T(8,128)(2,1)} %bitcast.14) | data formatting | bytes 2621440 | tf_op jit(solution)/shard_map/reshape | solution.py:87
  115.0 3.7 %copy.15 = bf16[80,64,128]{2,1,0:T(8,128)(2,1)} copy(bf16[80,64,128]{0,2,1:T(8,128)(2,1)} %bitcast.95) | data formatting | bytes 2621440
  (11 shorter events, 0.1 us)
Async XLA Ops:
  7.2 59.7 %copy-start = (bf16[32,256,128]{2,1,0:T(8,128)(2,1)S(1)}, bf16[32,256,128]{2,1,0:T(8,128)(2,1)}, u32[]{:S(2)}) copy-start(bf16[32,256,128]{2,1,0:T(8,128)(2,1)} %param.7) | copy-start | bytes 6291460
  7.2 8.4 %copy-start.2 = (f32[128,4]{0,1:T(4,128)S(1)}, f32[128,4]{0,1:T(4,128)}, u32[]{:S(2)}) copy-start(f32[128,4]{0,1:T(4,128)} %param.9) | copy-start | bytes 6148
  7.2 8.4 %copy-start.3 = (s32[128,4]{0,1:T(4,128)S(1)}, s32[128,4]{0,1:T(4,128)}, u32[]{:S(2)}) copy-start(s32[128,4]{0,1:T(4,128)} %param.8) | copy-start | bytes 6148
  7.2 8.6 %copy-start.1 = (bf16[256,32]{0,1:T(8,128)(2,1)S(1)}, bf16[256,32]{0,1:T(8,128)(2,1)}, u32[]{:S(2)}) copy-start(bf16[256,32]{0,1:T(8,128)(2,1)} %param.11) | copy-start | bytes 49156
  8.7 31.1 %collective-permute-start = (bf16[32,80,128]{2,1,0:T(8,128)(2,1)S(1)}, bf16[32,80,128]{2,1,0:T(8,128)(2,1)}, u32[]{:S(2)}, u32[]{:S(2)}) collective-permute-start(bf16[32,80,128]{2,1,0:T(8,128)(2,1)S(1)} %get-tuple-element.10), channel_id=1, source_target_pairs={{0,4},{4,8},{8,12},{12,16},{16,20},{20,24},{24,28},{28,0},{1,5},{5... | collective-permute-start | bytes 1966088 | tf_op jit(solution)/shard_map/ppermute | solution.py:18
  11.8 35.7 %collective-permute-start.1 = (bf16[32,80,128]{2,1,0:T(8,128)(2,1)S(1)}, bf16[32,80,128]{2,1,0:T(8,128)(2,1)}, u32[]{:S(2)}, u32[]{:S(2)}) collective-permute-start(bf16[32,80,128]{2,1,0:T(8,128)(2,1)S(1)} %get-tuple-element.9), channel_id=1, source_target_pairs={{4,0},{8,4},{12,8},{16,12},{20,16},{24,20},{28,24},{0,28},{5,1},{9... | collective-permute-start | bytes 1966088 | tf_op jit(solution)/shard_map/ppermute | solution.py:21
  77.6 33.8 %all-to-all-start = ((bf16[4,80,64,32]{1,3,2,0:T(8,128)(2,1)}), bf16[4,80,64,32]{1,3,2,0:T(8,128)(2,1)}, u32[]{:S(2)}, u32[]{:S(2)}) async-start(bf16[4,80,64,32]{1,3,2,0:T(8,128)(2,1)} %copy.12), calls=%async_computation | async-start | bytes 4194304 | tf_op jit(solution)/shard_map/all_to_all | solution.py:86
  82.1 27.9 %reduce-scatter.2.cloned.1.call-start = ((), (), s32[]{:S(2)}) async-start(), calls=%async_computation.2 | async-start | bytes 204800 | tf_op jit(solution)/shard_map/reduce_scatter | solution.py:88
Sparse Core Ops, SparseCore 0:
  87.5 22.4 reduce-scatter.1
